TPU v7x, 32 devices: a whole 2x2x4 slice. The times are simulated.
32 devices in a mesh: dp: 8 (over z, x), mp: 4 (over y, core).
Axes of the slice: x: 2, y: 2, z: 4, core: 2. Of those that a mesh axis runs over, the one named last changes fastest.
Arguments:
- patches: bfloat16 [8, 2048, 768], P('dp'), may hold values from -6 to 6
- cotangent: bfloat16 [8, 2048, 768], P('dp'), may hold values from -6 to 6
- keep_mask: int32 [8, 2048], P('dp'), may hold values from 0 to 1, as said below
- segment_ids: int32 [8, 2048], P('dp'), may hold values from 0 to 7, never falling along the last dimension, each value on 1 to 512 neighbouring positions
- step_count: int32 [1], replicated, may hold values from 2 to 8
- qkv_weight: float32 [3, 768, 768], P(None, None, 'mp'), may hold values from -0.21875 to 0.21875
- qkv_first: float32 [3, 768, 768], P(None, 'dp', 'mp'), may hold values from -0.00061035156 to 0.00061035156
- qkv_second: float32 [3, 768, 768], P(None, 'dp', 'mp'), may hold values from 7.4315953e-09 to 2.9669868e-08
- out_weight: float32 [768, 768], P('mp'), may hold values from -1.75 to 1.75
- out_first: float32 [768, 768], P('mp', 'dp'), may hold values from -0.00061035156 to 0.00061035156
- out_second: float32 [768, 768], P('mp', 'dp'), may hold values from 7.4315953e-09 to 2.9669868e-08
- up_weight: float32 [768, 3072], P(None, 'mp'), may hold values from -0.21875 to 0.21875
- up_first: float32 [768, 3072], P('dp', 'mp'), may hold values from -0.00061035156 to 0.00061035156
- up_second: float32 [768, 3072], P('dp', 'mp'), may hold values from 7.4315953e-09 to 2.9669868e-08
- down_weight: float32 [3072, 768], P('mp'), may hold values from -0.109375 to 0.109375
- down_first: float32 [3072, 768], P('mp', 'dp'), may hold values from -0.00061035156 to 0.00061035156
- down_second: float32 [3072, 768], P('mp', 'dp'), may hold values from 7.4315953e-09 to 2.9669868e-08
- head_params: float32 [5, 12, 64], P(None, 'mp'), may hold values from -2 to 2, as said below
- head_first: float32 [5, 12, 64], P(None, 'mp'), may hold values from -0.00061035156 to 0.00061035156
- head_second: float32 [5, 12, 64], P(None, 'mp'), may hold values from 7.4315953e-09 to 2.9669868e-08
- up_bias: float32 [3072], P('mp'), may hold values from -2 to 2
- upb_first: float32 [3072], P('mp'), may hold values from -0.00061035156 to 0.00061035156
- upb_second: float32 [3072], P('mp'), may hold values from 7.4315953e-09 to 2.9669868e-08
- vec_params: float32 [6, 768], replicated, may hold values from -2 to 2, as said below
- vec_first: float32 [6, 768], replicated, may hold values from -0.00061035156 to 0.00061035156
- vec_second: float32 [6, 768], replicated, may hold values from 7.4315953e-09 to 2.9669868e-08
Outputs:
- block_out: bfloat16 [8, 2048, 768], P('dp')
- grad_input: bfloat16 [8, 2048, 768], P('dp')
- new_qkv: float32 [3, 768, 768], P(None, 'dp', 'mp')
- new_qkv_first: float32 [3, 768, 768], P(None, 'dp', 'mp')
- new_qkv_second: float32 [3, 768, 768], P(None, 'dp', 'mp')
- new_out: float32 [768, 768], P('mp', 'dp')
- new_out_first: float32 [768, 768], P('mp', 'dp')
- new_out_second: float32 [768, 768], P('mp', 'dp')
- new_up: float32 [768, 3072], P('dp', 'mp')
- new_up_first: float32 [768, 3072], P('dp', 'mp')
- new_up_second: float32 [768, 3072], P('dp', 'mp')
- new_down: float32 [3072, 768], P('mp', 'dp')
- new_down_first: float32 [3072, 768], P('mp', 'dp')
- new_down_second: float32 [3072, 768], P('mp', 'dp')
- new_head: float32 [5, 12, 64], P(None, 'mp')
- new_head_first: float32 [5, 12, 64], P(None, 'mp')
- new_head_second: float32 [5, 12, 64], P(None, 'mp')
- new_upb: float32 [3072], P('mp')
- new_upb_first: float32 [3072], P('mp')
- new_upb_second: float32 [3072], P('mp')
- new_vec: float32 [6, 768], replicated
- new_vec_first: float32 [6, 768], replicated
- new_vec_second: float32 [6, 768], replicated
- grad_norm: float32 [1], replicated
- rms_stats: float32 [2], replicated
Inputs may be any that keep to these rules, and one draw needn't show every extreme that they name: `keep_mask`: per sequence each patch is kept with a chance from one half to all; the chance rises with the sequence index. `segment_ids`: within a row ids never fall; each image covers 1 to 512 consecutive slots, one exactly that many. `head_params`: rows 0 to 2 are biases, rows 3 and 4 gains. `vec_params`: rows 0 and 2 are gains, the others biases.
All inputs are finite; a program needn't handle non-finite values.
Results may differ from a plain program's by a relative error of at most 0.012.
Values sent between devices are 32-bit elements; how exact they have to be, the bound alone decides.
No kernel may reach another device: no remote copies, remote signals or barrier semaphores. Data moves between devices by JAX's collectives and lax.ppermute only.
A program may use at most 256 MiB of HBM per device.

v0:
```python
import jax
import jax.numpy as jnp
from jax import lax
from jax.sharding import PartitionSpec as P

NORM_EPS = 1e-06
CLIP_LIMIT = 1.0
LEARN_RATE = 0.1
BETA_ONE = 0.9
BETA_TWO = 0.95
ADAM_EPS = 1e-08
WEIGHT_DECAY = 0.1


def standardize(values):
    center = values - jnp.mean(values, axis=-1, keepdims=True)
    spread = jnp.mean(center * center, axis=-1, keepdims=True)
    factor = lax.rsqrt(spread + NORM_EPS)
    return (center * factor, factor)


def norm_back(grad_hat, normed, factor):
    return factor * (
        grad_hat
        - jnp.mean(grad_hat, axis=-1, keepdims=True)
        - normed * jnp.mean(grad_hat * normed, axis=-1, keepdims=True)
    )


def adam_step(weight, grad, first, second, factor, corr_one, corr_two, decay):
    grad = factor * grad
    first = BETA_ONE * first + (1.0 - BETA_ONE) * grad
    second = BETA_TWO * second + (1.0 - BETA_TWO) * grad * grad
    update = first / corr_one / (jnp.sqrt(second / corr_two) + ADAM_EPS)
    return (weight - LEARN_RATE * (update + decay * weight), first, second)


def local(
    patches,
    cotangent,
    keep_mask,
    segment_ids,
    step_count,
    qkv_weight,
    qkv_first,
    qkv_second,
    out_weight,
    out_first,
    out_second,
    up_weight,
    up_first,
    up_second,
    down_weight,
    down_first,
    down_second,
    head_params,
    head_first,
    head_second,
    up_bias,
    upb_first,
    upb_second,
    vec_params,
    vec_first,
    vec_second,
):
    seq_len = patches.shape[1]
    width = patches.shape[2]
    heads_here = head_params.shape[1]
    head_dim = head_params.shape[2]
    local_width = heads_here * head_dim
    head_scale = head_dim ** (-0.5)
    inputs = patches[0].astype(jnp.float32)
    keep_row = keep_mask[0]
    seg_row = segment_ids[0]
    keep_f = keep_row.astype(jnp.float32)
    places = jnp.arange(seq_len)
    xh_first, rs_first = standardize(inputs)
    a_first = (xh_first * vec_params[0] + vec_params[1]).astype(jnp.bfloat16)
    qkv_low = qkv_weight.astype(jnp.bfloat16)
    raw = jnp.einsum("sd,kde->kse", a_first, qkv_low, preferred_element_type=jnp.float32)
    raw = raw + head_params[0:3].reshape(3, 1, local_width)
    query = raw[0].reshape(seq_len, heads_here, head_dim)
    key_raw = raw[1].reshape(seq_len, heads_here, head_dim)
    value = raw[2].reshape(seq_len, heads_here, head_dim)
    q_hat, q_factor = standardize(query)
    k_hat, k_factor = standardize(key_raw)
    q_in = (q_hat * head_params[3] * head_scale).astype(jnp.bfloat16)
    k_in = (k_hat * head_params[4]).astype(jnp.bfloat16)
    v_in = value.astype(jnp.bfloat16)
    block = min(512, seq_len)
    blocks = seq_len // block

    def block_scores(start):
        q_block = q_in[start : start + block]
        scores = jnp.einsum("qhd,khd->hqk", q_block, k_in, preferred_element_type=jnp.float32)
        allowed = (seg_row[start : start + block, None] == seg_row[None, :]) & (
            (keep_row[None, :] == 1) | (places[start : start + block, None] == places[None, :])
        )
        return (jnp.where(allowed[None], scores, -1e30), q_block)

    outs_list = []
    lse_list = []
    for index in range(blocks):
        scores, q_block = block_scores(index * block)
        top = jnp.max(scores, axis=-1, keepdims=True)
        expo = jnp.exp(scores - top)
        total = jnp.sum(expo, axis=-1, keepdims=True)
        probs = (expo / total).astype(jnp.bfloat16)
        lse_list.append(top + jnp.log(total))
        outs_list.append(
            jnp.einsum("hqk,khd->qhd", probs, v_in, preferred_element_type=jnp.float32)
        )
    mixed = jnp.concatenate(outs_list, axis=0).reshape(seq_len, local_width).astype(jnp.bfloat16)
    out_low = out_weight.astype(jnp.bfloat16)
    attn = (
        lax.psum(jnp.dot(mixed, out_low, preferred_element_type=jnp.float32), "mp") + vec_params[4]
    )
    hidden = inputs + attn
    xh_second, rs_second = standardize(hidden)
    a_second = (xh_second * vec_params[2] + vec_params[3]).astype(jnp.bfloat16)
    up_low = up_weight.astype(jnp.bfloat16)
    upper = jnp.dot(a_second, up_low, preferred_element_type=jnp.float32) + up_bias
    gelu_value, gelu_back = jax.vjp(lambda val: jax.nn.gelu(val, approximate=False), upper)
    gated = gelu_value.astype(jnp.bfloat16)
    down_low = down_weight.astype(jnp.bfloat16)
    mlp = (
        lax.psum(jnp.dot(gated, down_low, preferred_element_type=jnp.float32), "mp") + vec_params[5]
    )
    result = hidden + mlp
    count_here = jnp.sum(keep_f)
    attn_sq = jnp.sum(keep_f[:, None] * attn * attn)
    mlp_sq = jnp.sum(keep_f[:, None] * mlp * mlp)
    count, attn_total, mlp_total = lax.psum((count_here, attn_sq, mlp_sq), "dp")
    grad_out = cotangent[0].astype(jnp.float32) * keep_f[:, None]
    grad_mlp = grad_out.astype(jnp.bfloat16)
    grad_bdown = jnp.sum(grad_mlp.astype(jnp.float32), axis=0)
    grad_down = jnp.einsum("sf,sd->fd", gated, grad_mlp, preferred_element_type=jnp.float32)
    grad_gated = jnp.einsum("sd,fd->sf", grad_mlp, down_low, preferred_element_type=jnp.float32)
    grad_upper = gelu_back(grad_gated)[0].astype(jnp.bfloat16)
    grad_bup = jnp.sum(grad_upper.astype(jnp.float32), axis=0)
    grad_up = jnp.einsum("sd,sf->df", a_second, grad_upper, preferred_element_type=jnp.float32)
    grad_xn2 = lax.psum(
        jnp.einsum("sf,df->sd", grad_upper, up_low, preferred_element_type=jnp.float32), "mp"
    )
    grad_gain2 = jnp.sum(grad_xn2 * xh_second, axis=0)
    grad_bias2 = jnp.sum(grad_xn2, axis=0)
    grad_hidden = grad_out + norm_back(grad_xn2 * vec_params[2], xh_second, rs_second)
    grad_attn = grad_hidden.astype(jnp.bfloat16)
    grad_bout = jnp.sum(grad_attn.astype(jnp.float32), axis=0)
    grad_outw = jnp.einsum("se,sd->ed", mixed, grad_attn, preferred_element_type=jnp.float32)
    grad_mixed = jnp.einsum("sd,ed->se", grad_attn, out_low, preferred_element_type=jnp.float32)
    grad_mixed = grad_mixed.astype(jnp.bfloat16).reshape(seq_len, heads_here, head_dim)
    grad_kin = jnp.zeros((seq_len, heads_here, head_dim), jnp.float32)
    grad_vin = jnp.zeros((seq_len, heads_here, head_dim), jnp.float32)
    grad_qlist = []
    for index in range(blocks):
        start = index * block
        scores, q_block = block_scores(start)
        probs_full = jnp.exp(scores - lse_list[index])
        probs = probs_full.astype(jnp.bfloat16)
        grad_block = grad_mixed[start : start + block]
        grad_vin = grad_vin + jnp.einsum(
            "hqk,qhd->khd", probs, grad_block, preferred_element_type=jnp.float32
        )
        grad_probs = jnp.einsum(
            "qhd,khd->hqk", grad_block, v_in, preferred_element_type=jnp.float32
        )
        delta = jnp.sum(probs_full * grad_probs, axis=-1, keepdims=True)
        grad_scores = (probs_full * (grad_probs - delta)).astype(jnp.bfloat16)
        grad_qlist.append(
            jnp.einsum("hqk,khd->qhd", grad_scores, k_in, preferred_element_type=jnp.float32)
        )
        grad_kin = grad_kin + jnp.einsum(
            "hqk,qhd->khd", grad_scores, q_block, preferred_element_type=jnp.float32
        )
    grad_qin = jnp.concatenate(grad_qlist, axis=0) * head_scale
    grad_qgain = jnp.sum(grad_qin * q_hat, axis=0)
    grad_query = norm_back(grad_qin * head_params[3], q_hat, q_factor)
    grad_kgain = jnp.sum(grad_kin * k_hat, axis=0)
    grad_key = norm_back(grad_kin * head_params[4], k_hat, k_factor)
    grad_raw = jnp.stack(
        [
            grad_query.reshape(seq_len, local_width),
            grad_key.reshape(seq_len, local_width),
            grad_vin.reshape(seq_len, local_width),
        ]
    ).astype(jnp.bfloat16)
    grad_bqkv = jnp.sum(grad_raw.astype(jnp.float32), axis=1)
    grad_qkv = jnp.einsum("sd,kse->kde", a_first, grad_raw, preferred_element_type=jnp.float32)
    grad_xn1 = lax.psum(
        jnp.einsum("kse,kde->sd", grad_raw, qkv_low, preferred_element_type=jnp.float32), "mp"
    )
    grad_gain1 = jnp.sum(grad_xn1 * xh_first, axis=0)
    grad_bias1 = jnp.sum(grad_xn1, axis=0)
    grad_inputs = grad_hidden + norm_back(grad_xn1 * vec_params[0], xh_first, rs_first)
    vec_grad = jnp.stack([grad_gain1, grad_bias1, grad_gain2, grad_bias2, grad_bout, grad_bdown])
    head_grad = jnp.concatenate(
        [grad_bqkv.reshape(3, heads_here, head_dim), jnp.stack([grad_qgain, grad_kgain])], axis=0
    )
    vec_grad, head_grad, bup_grad = lax.psum((vec_grad, head_grad, grad_bup), "dp")
    dp_rank = lax.axis_index("dp")
    rows = width // lax.axis_size("dp")
    start_row = dp_rank * rows
    summed = lax.psum((grad_qkv, grad_outw, grad_up, grad_down), "dp")
    shares = (
        lax.dynamic_slice_in_dim(summed[0], start_row, rows, 1),
        lax.dynamic_slice_in_dim(summed[1], start_row, rows, 1),
        lax.dynamic_slice_in_dim(summed[2], start_row, rows, 0),
        lax.dynamic_slice_in_dim(summed[3], start_row, rows, 1),
    )
    old_shares = (
        lax.dynamic_slice_in_dim(qkv_weight, start_row, rows, 1),
        lax.dynamic_slice_in_dim(out_weight, start_row, rows, 1),
        lax.dynamic_slice_in_dim(up_weight, start_row, rows, 0),
        lax.dynamic_slice_in_dim(down_weight, start_row, rows, 1),
    )
    first_dp = dp_rank == 0
    first_mp = lax.axis_index("mp") == 0
    big_sq = sum((jnp.sum(share * share) for share in shares))
    split_sq = jnp.sum(head_grad * head_grad) + jnp.sum(bup_grad * bup_grad)
    whole_sq = jnp.sum(vec_grad * vec_grad)
    raw_sq = (
        big_sq + jnp.where(first_dp, split_sq, 0.0) + jnp.where(first_dp & first_mp, whole_sq, 0.0)
    )
    sq_total = lax.psum(raw_sq, ("dp", "mp"))
    scale = seq_len * lax.axis_size("dp") / count
    grad_norm = scale * jnp.sqrt(sq_total)
    factor = jnp.minimum(1.0, CLIP_LIMIT / (grad_norm + 1e-06)) * scale
    steps_f = step_count[0].astype(jnp.float32)
    corr_one = 1.0 - BETA_ONE**steps_f
    corr_two = 1.0 - BETA_TWO**steps_f
    new_qkv = adam_step(
        old_shares[0], shares[0], qkv_first, qkv_second, factor, corr_one, corr_two, WEIGHT_DECAY
    )
    new_out = adam_step(
        old_shares[1], shares[1], out_first, out_second, factor, corr_one, corr_two, WEIGHT_DECAY
    )
    new_up = adam_step(
        old_shares[2], shares[2], up_first, up_second, factor, corr_one, corr_two, WEIGHT_DECAY
    )
    new_down = adam_step(
        old_shares[3], shares[3], down_first, down_second, factor, corr_one, corr_two, WEIGHT_DECAY
    )
    new_head = adam_step(
        head_params, head_grad, head_first, head_second, factor, corr_one, corr_two, 0.0
    )
    new_upb = adam_step(up_bias, bup_grad, upb_first, upb_second, factor, corr_one, corr_two, 0.0)
    new_vec = adam_step(
        vec_params, vec_grad, vec_first, vec_second, factor, corr_one, corr_two, 0.0
    )
    rms = jnp.sqrt(jnp.stack([attn_total, mlp_total]) / (count * width))
    return (
        result.astype(jnp.bfloat16)[None],
        (grad_inputs * scale).astype(jnp.bfloat16)[None],
        new_qkv[0],
        new_qkv[1],
        new_qkv[2],
        new_out[0],
        new_out[1],
        new_out[2],
        new_up[0],
        new_up[1],
        new_up[2],
        new_down[0],
        new_down[1],
        new_down[2],
        new_head[0],
        new_head[1],
        new_head[2],
        new_upb[0],
        new_upb[1],
        new_upb[2],
        new_vec[0],
        new_vec[1],
        new_vec[2],
        grad_norm.reshape(1),
        rms,
    )


def solution(mesh):
    placed = (
        P("dp", None, None),
        P("dp", None, None),
        P("dp", None),
        P("dp", None),
        P(),
        P(None, None, "mp"),
        P(None, "dp", "mp"),
        P(None, "dp", "mp"),
        P("mp", None),
        P("mp", "dp"),
        P("mp", "dp"),
        P(None, "mp"),
        P("dp", "mp"),
        P("dp", "mp"),
        P("mp", None),
        P("mp", "dp"),
        P("mp", "dp"),
        P(None, "mp", None),
        P(None, "mp", None),
        P(None, "mp", None),
        P("mp"),
        P("mp"),
        P("mp"),
        P(),
        P(),
        P(),
    )
    return jax.shard_map(
        local,
        mesh=mesh,
        in_specs=placed,
        out_specs=(
            P("dp", None, None),
            P("dp", None, None),
            P(None, "dp", "mp"),
            P(None, "dp", "mp"),
            P(None, "dp", "mp"),
            P("mp", "dp"),
            P("mp", "dp"),
            P("mp", "dp"),
            P("dp", "mp"),
            P("dp", "mp"),
            P("dp", "mp"),
            P("mp", "dp"),
            P("mp", "dp"),
            P("mp", "dp"),
            P(None, "mp", None),
            P(None, "mp", None),
            P(None, "mp", None),
            P("mp"),
            P("mp"),
            P("mp"),
            P(),
            P(),
            P(),
            P(),
            P(),
        ),
        check_vma=False,
    )
```

profile of v0, /device:TPU:0, one launch (start us, length us, event | category | flops | bytes accessed | tf_op | source)
XLA Modules:
  0.0 1091.9 jit_solution(17115793789987397871)
XLA Ops:
  9.6 2.5 convert_reduce_fusion
  12.1 2.9 fusion.25
  15.8 2.3 fusion.148
  31.1 2.0 multiply_convert_fusion.6
  33.1 6.5 fusion.61
  39.7 6.6 select_reduce_fusion
  46.4 6.6 select_reduce_fusion.1
  53.0 7.8 fusion.3
  60.9 6.6 fusion.97
  67.5 7.8 fusion.2
  75.3 6.4 fusion.96
  81.7 6.7 select_reduce_fusion.2
  88.4 7.8 fusion.1
  96.1 6.6 fusion.95
  102.8 6.8 select_reduce_fusion.3
  109.6 7.8 fusion
  117.4 6.5 fusion.94
  124.8 3.6 fusion.126
  128.6 122.4 %all-reduce.8.cloned.1.call-done = f32[2048,768]{1,0:T(8,128)} async-done(((f32[2048,768]{1,0:T(8,128)}), f32[2048,768]{1,0:T(8,128)}) %all-reduce.8.cloned.1.call-update) | async-done | bytes 6291472 | tf_op jit(solution)/shard_map/psum | solution.py:116
  250.9 3.7 fusion.159
  258.5 17.7 %multiply_convert_fusion.4 = (bf16[2048,768]{1,0:T(8,128)(2,1)}, f32[2048,768]{1,0:T(8,128)}, f32[2048,768]{1,0:T(8,128)}) fusion(f32[768]{0:T(1024)S(1)} %copy-done.103, bf16[2048,768]{1,0:T(8,128)(2,1)S(1)} %add_convert_fusion.2, f32[768,768]{1,0:T(8,128)S(1)} %copy-done.84), kind=kOutput, calls=%fused_computation.76 | convolution fusion | flops 2520317952 | bytes 21236736 | tf_op jit(solution)/shard_map/dot_general | solution.py:122
  276.2 8.2 convert_reduce_fusion.3
  286.0 4.5 fusion.105
  293.8 8.1 fusion.101
  301.8 108.6 %all-reduce.10.cloned.1.call-done = f32[2048,768]{1,0:T(8,128)} async-done(((f32[2048,768]{1,0:T(8,128)}), f32[2048,768]{1,0:T(8,128)}) %all-reduce.10.cloned.1.call-update) | async-done | bytes 6291472 | tf_op jit(solution)/shard_map/psum | solution.py:142
  410.5 6.8 multiply_reduce_fusion.4
  417.3 6.5 convert_reduce_fusion.2
  426.7 6.8 multiply_reduce_fusion.3
  433.6 10.1 multiply_convert_fusion.3
  443.7 5.0 fusion.164
  448.7 3.3 fusion.121
  452.1 4.3 fusion.30
  456.4 9.1 multiply_reduce_fusion.2
  465.6 5.7 fusion.28
  471.3 7.4 multiply_reduce_fusion.1
  478.7 10.3 fusion.76
  489.0 9.2 multiply_reduce_fusion
  498.2 5.9 fusion.82
  504.1 9.6 multiply_convert_fusion
  513.7 5.7 fusion.167
  519.3 10.3 multiply_convert_fusion.2
  529.6 2.8 fusion.165
  532.4 4.1 convolution_add_fusion.2
  536.5 3.6 multiply_convert_fusion.1
  540.2 2.0 fusion.166
  545.1 2.6 multiply_reduce_fusion.9
  548.8 3.3 fusion.85
  553.0 4.5 convolution_bitcast_fusion
  557.9 7.1 fusion.168
  565.0 4.1 fusion.144
  572.0 3.6 fusion.87
  580.0 2.0 constant_dynamic-slice_fusion
  582.1 1.9 copy.57
  589.1 2.6 multiply_reduce_fusion.10
  592.4 2.0 convert_reduce_fusion.4
  595.2 183.8 %all-reduce.14.cloned.1.call-done = (f32[2048,768]{1,0:T(8,128)}, f32[2048,768]{1,0:T(8,128)}) async-done(((f32[2048,768]{1,0:T(8,128)}, f32[2048,768]{1,0:T(8,128)}), (f32[2048,768]{1,0:T(8,128)}, f32[2048,768]{1,0:T(8,128)})) %all-reduce.14.cloned.1.call-update) | async-done | bytes 12582928 | tf_op jit(solution)/shard_map/psum | solution.py:127
  779.0 16.2 %fusion.24 = (f32[768]{0:T(1024)S(1)}, f32[2048]{0:T(1024)S(1)}, f32[2048]{0:T(1024)S(1)}, f32[768]{0:T(1024)S(1)}, bf16[1,2048,768]{2,1,0:T(8,128)(2,1)}, /*index=5*/f32[]{:T(128)}, f32[768]{0:T(1024)S(1)}, f32[]{:T(128)}) fusion(f32[2048,768]{1,0:T(8,128)} %get-tuple-element.83, bf16[1,2048,768]{2,1,0:T(8,128)(2,1)S(1)} %copy-done.6, ...), kind=kLoop, calls=%fused_computation.53 | loop fusion | flops 39315200 | bytes 34662408 | tf_op jit(solution)/shard_map/reduce_sum | solution.py:193
  795.3 41.8 %all-reduce = (f32[]{:T(128)}, f32[5,3,64]{2,1,0:T(4,128)S(1)}, f32[768]{0:T(1024)S(1)}, f32[6,768]{1,0:T(8,128)S(1)}, f32[1]{0:T(128)}, /*index=5*/f32[1]{0:T(128)}) all-reduce(f32[]{:T(128)} %convert_reduce_fusion.5, f32[5,3,64]{2,1,0:T(4,128)S(1)} %pad_maximum_fusion.3, ...), channel_id=1, replica_groups=mesh['dp'=8,'mp'=4] {'dp'}, use_global_device_ids=true, to_apply=%region_33.34 | all-reduce | flops 6339 | bytes 50712 | tf_op jit(solution)/shard_map/psum | solution.py:133
  842.2 7.1 fusion.71
  849.4 171.1 %all-reduce.12.cloned.1.call-done = (f32[3,768,192]{1,2,0:T(8,128)}, f32[192,768]{1,0:T(8,128)}, f32[768,768]{1,0:T(8,128)}, f32[768,768]{0,1:T(8,128)}) async-done(((f32[3,768,192]{1,2,0:T(8,128)}, f32[192,768]{1,0:T(8,128)}, f32[768,768]{1,0:T(8,128)}, f32[768,768]{0,1:T(8,128)}), (f32[3,768,192]{1,2,0:T(8,128)}, f32[192,768]{1,0:T(8,128)}, f32[768,768]{1,0:T(8,128)}, ...) | async-done | bytes 7077904 | tf_op jit(solution)/shard_map/psum | solution.py:204
  1029.8 1.9 fusion.132
  1031.7 39.1 %psum.117 = f32[]{:T(128)} all-reduce(f32[]{:T(128)S(6)} %add.375), channel_id=1, replica_groups=mesh['dp'=8,'mp'=4] {'dp','mp'}, use_global_device_ids=true, to_apply=%region_58.59 | all-reduce | flops 1 | bytes 8 | tf_op jit(solution)/shard_map/psum | solution.py:225
  1075.9 2.3 multiply_subtract_fusion.1
  1081.9 2.0 multiply_subtract_fusion
  (354 shorter events, 63.6 us)
Async XLA Ops:
  7.2 8.6 copy-start.5
  7.2 7.8 copy-start.68
  7.2 243.7 %all-reduce.8.cloned.1.call-start = ((), (), s32[]{:S(2)}) async-start(), calls=%async_computation | async-start | bytes 12582912 | tf_op jit(solution)/shard_map/psum | solution.py:116
  9.5 21.7 %copy-start.70 = (f32[3,64]{1,0:T(4,128)}, f32[3,64]{1,0:T(4,128)S(1)}, u32[]{:S(2)}) copy-start(f32[3,64]{1,0:T(4,128)S(1)} %get-tuple-element.122) | copy-start | bytes 2308
  15.7 235.2 %copy-start.85 = (f32[768]{0:T(1024)}, f32[768]{0:T(1024)S(1)}, u32[]{:S(2)}) copy-start(f32[768]{0:T(1024)S(1)} %get-tuple-element.66) | copy-start | bytes 9220
  24.5 15.2 %copy-start.56 = (f32[2048,3]{0,1:T(4,128)}, f32[2048,3]{0,1:T(4,128)S(1)}, u32[]{:S(2)}) copy-start(f32[2048,3]{0,1:T(4,128)S(1)} %broadcast_multiply_fusion.5) | copy-start | bytes 73732
  26.2 20.2 %copy-start.58 = (f32[2048,3]{0,1:T(4,128)}, f32[2048,3]{0,1:T(4,128)S(1)}, u32[]{:S(2)}) copy-start(f32[2048,3]{0,1:T(4,128)S(1)} %add_rsqrt_fusion.1) | copy-start | bytes 73732
  27.7 18.6 %copy-start.48 = (f32[2048,3]{0,1:T(4,128)}, f32[2048,3]{0,1:T(4,128)S(1)}, u32[]{:S(2)}) copy-start(f32[2048,3]{0,1:T(4,128)S(1)} %broadcast_multiply_fusion.4) | copy-start | bytes 73732
  29.4 16.9 %copy-start.50 = (f32[2048,3]{0,1:T(4,128)}, f32[2048,3]{0,1:T(4,128)S(1)}, u32[]{:S(2)}) copy-start(f32[2048,3]{0,1:T(4,128)S(1)} %add_rsqrt_fusion) | copy-start | bytes 73732
  31.1 71.7 %copy-start.29 = (bf16[2048,3,64]{0,2,1:T(8,128)(2,1)}, bf16[2048,3,64]{0,2,1:T(8,128)(2,1)S(1)}, u32[]{:S(2)}) copy-start(bf16[2048,3,64]{0,2,1:T(8,128)(2,1)S(1)} %multiply_convert_fusion.7) | copy-start | bytes 2359300
  33.1 69.7 %copy-start.2 = (bf16[2048,3,64]{0,2,1:T(8,128)(2,1)}, bf16[2048,3,64]{0,2,1:T(8,128)(2,1)S(1)}, u32[]{:S(2)}) copy-start(bf16[2048,3,64]{0,2,1:T(8,128)(2,1)S(1)} %multiply_convert_fusion.6) | copy-start | bytes 2359300
  39.7 21.2 %copy-start.13 = (pred[512,2048]{1,0:T(8,128)(4,1)}, pred[512,2048]{1,0:T(8,128)(4,1)S(1)}, u32[]{:S(2)}) copy-start(pred[512,2048]{1,0:T(8,128)(4,1)S(1)} %get-tuple-element.126) | copy-start | bytes 3145732
  39.7 35.6 %copy-start.7 = (pred[512,2048]{1,0:T(8,128)(4,1)}, pred[512,2048]{1,0:T(8,128)(4,1)S(1)}, u32[]{:S(2)}) copy-start(pred[512,2048]{1,0:T(8,128)(4,1)S(1)} %get-tuple-element.125) | copy-start | bytes 3145732
  39.7 56.5 %copy-start.10 = (pred[512,2048]{1,0:T(8,128)(4,1)}, pred[512,2048]{1,0:T(8,128)(4,1)S(1)}, u32[]{:S(2)}) copy-start(pred[512,2048]{1,0:T(8,128)(4,1)S(1)} %get-tuple-element.124) | copy-start | bytes 3145732
  39.7 77.7 %copy-start.15 = (pred[512,2048]{1,0:T(8,128)(4,1)}, pred[512,2048]{1,0:T(8,128)(4,1)S(1)}, u32[]{:S(2)}) copy-start(pred[512,2048]{1,0:T(8,128)(4,1)S(1)} %get-tuple-element.123) | copy-start | bytes 3145732
  46.3 14.5 %copy-start.77 = (f32[3,512]{1,0:T(4,128)}, f32[3,512]{1,0:T(4,128)S(1)}, u32[]{:S(2)}) copy-start(f32[3,512]{1,0:T(4,128)S(1)} %get-tuple-element.131) | copy-start | bytes 18436
  53.0 7.9 copy-start.20
  128.5 282.0 %all-reduce.10.cloned.1.call-start = ((), (), s32[]{:S(2)}) async-start(), calls=%async_computation.1 | async-start | bytes 12582912 | tf_op jit(solution)/shard_map/psum | solution.py:142
  128.6 288.7 %copy-start.74 = (f32[1,2048]{1,0:T(1,128)}, f32[1,2048]{1,0:T(1,128)S(1)}, u32[]{:S(2)}) copy-start(f32[1,2048]{1,0:T(1,128)S(1)} %convert_element_type.148) | copy-start | bytes 24580
  258.5 17.7 %copy-start.41 = (bf16[2048,768]{1,0:T(8,128)(2,1)}, bf16[2048,768]{1,0:T(8,128)(2,1)S(1)}, u32[]{:S(2)}) copy-start(bf16[2048,768]{1,0:T(8,128)(2,1)S(1)} %add_convert_fusion.2) | copy-start | bytes 9437188
  258.5 17.7 %copy-start.25 = (bf16[1,2048,768]{2,1,0:T(8,128)(2,1)S(1)}, bf16[1,2048,768]{2,1,0:T(8,128)(2,1)}, u32[]{:S(2)}) copy-start(bf16[1,2048,768]{2,1,0:T(8,128)(2,1)} %param.27) | copy-start | bytes 9437188
  258.5 17.7 %copy-start.79 = (f32[768,768]{1,0:T(8,128)S(1)}, f32[768,768]{1,0:T(8,128)}, u32[]{:S(2)}) copy-start(f32[768,768]{1,0:T(8,128)} %param.40) | copy-start | bytes 7077892
  290.5 488.4 %all-reduce.14.cloned.1.call-start = ((), (), s32[]{:S(2)}) async-start(), calls=%async_computation.3 | async-start | bytes 25165824 | tf_op jit(solution)/shard_map/psum | solution.py:127
  293.8 139.8 %copy-start.61 = (f32[3,512]{1,0:T(4,128)}, f32[3,512]{1,0:T(4,128)S(1)}, u32[]{:S(2)}) copy-start(f32[3,512]{1,0:T(4,128)S(1)} %log_add_fusion.3) | copy-start | bytes 18436
  417.3 9.4 slice-start.9
  417.3 9.4 slice-start.10
  417.3 9.4 slice-start.11
  426.7 25.3 %slice-start.6 = ((s8[12582912]{0:T(1024)(128)(4,1)}), s8[4194304]{0:T(1024)(128)(4,1)S(1)}, s32[]{:S(2)}) async-start(s8[12582912]{0:T(1024)(128)(4,1)} %bitcast.194), calls=%async_computation.10 | async-start | bytes 8388608
  426.7 25.3 %slice-start.7 = ((s8[12582912]{0:T(1024)(128)(4,1)}), s8[4194304]{0:T(1024)(128)(4,1)S(1)}, s32[]{:S(2)}) async-start(s8[12582912]{0:T(1024)(128)(4,1)} %bitcast.194), calls=%async_computation.11 | async-start | bytes 8388608
  433.6 10.2 copy-start.3
  433.6 18.5 %slice-start.8 = ((s8[12582912]{0:T(1024)(128)(4,1)}), s8[4194304]{0:T(1024)(128)(4,1)S(1)}, s32[]{:S(2)}) async-start(s8[12582912]{0:T(1024)(128)(4,1)} %bitcast.194), calls=%async_computation.12 | async-start | bytes 8388608
  443.7 8.3 copy-start.11
  443.7 8.4 copy-start.47
  452.1 13.4 %slice-start = ((s8[12582912]{0:T(1024)(128)(4,1)}), s8[4194304]{0:T(1024)(128)(4,1)S(1)}, s32[]{:S(2)}) async-start(s8[12582912]{0:T(1024)(128)(4,1)} %bitcast.190), calls=%async_computation.4 | async-start | bytes 8388608
  456.4 9.1 slice-start.1
  456.4 9.1 slice-start.2
  471.3 17.7 %slice-start.3 = ((s8[12582912]{0:T(1024)(128)(4,1)}), s8[4194304]{0:T(1024)(128)(4,1)S(1)}, s32[]{:S(2)}) async-start(s8[12582912]{0:T(1024)(128)(4,1)} %bitcast.192), calls=%async_computation.7 | async-start | bytes 8388608
  471.3 17.7 %slice-start.4 = ((s8[12582912]{0:T(1024)(128)(4,1)}), s8[4194304]{0:T(1024)(128)(4,1)S(1)}, s32[]{:S(2)}) async-start(s8[12582912]{0:T(1024)(128)(4,1)} %bitcast.192), calls=%async_computation.8 | async-start | bytes 8388608
  478.7 10.3 slice-start.5
  504.1 9.6 copy-start.4
  519.3 17.2 %slice-start.14 = ((s8[12582912]{0:T(1024)(128)(4,1)}), s8[4194304]{0:T(1024)(128)(4,1)S(1)}, s32[]{:S(2)}) async-start(s8[12582912]{0:T(1024)(128)(4,1)} %bitcast.200), calls=%async_computation.18 | async-start | bytes 8388608
  519.3 17.2 %slice-start.15 = ((s8[12582912]{0:T(1024)(128)(4,1)}), s8[4194304]{0:T(1024)(128)(4,1)S(1)}, s32[]{:S(2)}) async-start(s8[12582912]{0:T(1024)(128)(4,1)} %bitcast.200), calls=%async_computation.19 | async-start | bytes 8388608
  557.6 462.9 %all-reduce.12.cloned.1.call-start = ((), (), s32[]{:S(2)}) async-start(), calls=%async_computation.2 | async-start | bytes 14155776 | tf_op jit(solution)/shard_map/psum | solution.py:204
  557.9 11.3 %slice-start.12 = ((s8[6291456]{0:T(1024)(128)(4,1)}), s8[4194304]{0:T(1024)(128)(4,1)S(1)}, s32[]{:S(2)}) async-start(s8[6291456]{0:T(1024)(128)(4,1)} %bitcast.198), calls=%async_computation.16 | async-start | bytes 8388608
  779.0 16.2 %copy-start.94 = (f32[1,768]{1,0:T(1,128)S(1)}, f32[1,768]{1,0:T(1,128)}, u32[]{:S(2)}) copy-start(f32[1,768]{1,0:T(1,128)} %stack.45) | copy-start | bytes 9220
  779.0 16.2 %copy-start.95 = (f32[1,768]{1,0:T(1,128)S(1)}, f32[1,768]{1,0:T(1,128)}, u32[]{:S(2)}) copy-start(f32[1,768]{1,0:T(1,128)} %stack.46) | copy-start | bytes 9220
  779.0 16.2 %copy-start.96 = (f32[1,768]{1,0:T(1,128)S(1)}, f32[1,768]{1,0:T(1,128)}, u32[]{:S(2)}) copy-start(f32[1,768]{1,0:T(1,128)} %stack.47) | copy-start | bytes 9220
  779.0 16.3 %copy-start.102 = (f32[768]{0:T(1024)S(1)}, f32[768]{0:T(1024)}, u32[]{:S(2)}) copy-start(f32[768]{0:T(1024)} %get-tuple-element.149) | copy-start | bytes 9220
  779.0 63.2 %copy-start.83 = (f32[768]{0:T(1024)S(1)}, f32[768]{0:T(1024)}, u32[]{:S(2)}) copy-start(f32[768]{0:T(1024)} %copy-done.81) | copy-start | bytes 9220
  842.2 229.4 %copy-start.52 = (f32[3,96,192]{1,2,0:T(8,128)S(1)}, f32[3,96,192]{1,2,0:T(8,128)}, u32[]{:S(2)}) copy-start(f32[3,96,192]{1,2,0:T(8,128)} %copy.51) | copy-start | bytes 663556
  849.3 228.9 %copy-start.66 = (f32[192,96]{1,0:T(8,128)S(1)}, f32[192,96]{1,0:T(8,128)}, u32[]{:S(2)}) copy-start(f32[192,96]{1,0:T(8,128)} %param.36) | copy-start | bytes 221188
  849.3 228.9 %copy-start.67 = (f32[192,96]{1,0:T(8,128)S(1)}, f32[192,96]{1,0:T(8,128)}, u32[]{:S(2)}) copy-start(f32[192,96]{1,0:T(8,128)} %param.35) | copy-start | bytes 221188
  849.3 230.7 %copy-start.104 = (f32[768]{0:T(1024)S(1)}, f32[768]{0:T(1024)}, u32[]{:S(2)}) copy-start(f32[768]{0:T(1024)} %param.46) | copy-start | bytes 9220
  849.3 230.7 %copy-start.105 = (f32[768]{0:T(1024)S(1)}, f32[768]{0:T(1024)}, u32[]{:S(2)}) copy-start(f32[768]{0:T(1024)} %param.48) | copy-start | bytes 9220
  849.3 230.7 %copy-start.106 = (f32[768]{0:T(1024)S(1)}, f32[768]{0:T(1024)}, u32[]{:S(2)}) copy-start(f32[768]{0:T(1024)} %param.47) | copy-start | bytes 9220
  849.3 231.3 %copy-start.80 = (f32[5,3,64]{2,1,0:T(4,128)S(1)}, f32[5,3,64]{2,1,0:T(4,128)}, u32[]{:S(2)}) copy-start(f32[5,3,64]{2,1,0:T(4,128)} %param.43) | copy-start | bytes 11524
  849.3 231.3 %copy-start.97 = (f32[5,3,64]{2,1,0:T(4,128)S(1)}, f32[5,3,64]{2,1,0:T(4,128)}, u32[]{:S(2)}) copy-start(f32[5,3,64]{2,1,0:T(4,128)} %param.45) | copy-start | bytes 11524
  849.3 231.3 %copy-start.98 = (f32[5,3,64]{2,1,0:T(4,128)S(1)}, f32[5,3,64]{2,1,0:T(4,128)}, u32[]{:S(2)}) copy-start(f32[5,3,64]{2,1,0:T(4,128)} %param.44) | copy-start | bytes 11524
  849.3 231.9 %copy-start.69 = (f32[6,768]{1,0:T(8,128)S(1)}, f32[6,768]{1,0:T(8,128)}, u32[]{:S(2)}) copy-start(f32[6,768]{1,0:T(8,128)} %param.49) | copy-start | bytes 55300
  849.3 231.9 %copy-start.92 = (f32[6,768]{1,0:T(8,128)S(1)}, f32[6,768]{1,0:T(8,128)}, u32[]{:S(2)}) copy-start(f32[6,768]{1,0:T(8,128)} %param.51) | copy-start | bytes 55300
  849.4 231.9 %copy-start.93 = (f32[6,768]{1,0:T(8,128)S(1)}, f32[6,768]{1,0:T(8,128)}, u32[]{:S(2)}) copy-start(f32[6,768]{1,0:T(8,128)} %param.50) | copy-start | bytes 55300
  849.4 232.5 %copy-start.53 = (f32[768,96]{0,1:T(8,128)S(1)}, f32[768,96]{0,1:T(8,128)}, u32[]{:S(2)}) copy-start(f32[768,96]{0,1:T(8,128)} %copy.57) | copy-start | bytes 884740
  849.4 232.5 %copy-start.62 = (f32[768,96]{0,1:T(8,128)S(1)}, f32[768,96]{0,1:T(8,128)}, u32[]{:S(2)}) copy-start(f32[768,96]{0,1:T(8,128)} %param.42) | copy-start | bytes 884740
  849.4 232.5 %copy-start.63 = (f32[768,96]{0,1:T(8,128)S(1)}, f32[768,96]{0,1:T(8,128)}, u32[]{:S(2)}) copy-start(f32[768,96]{0,1:T(8,128)} %param.41) | copy-start | bytes 884740
  (70 other events, 271.3 us)
Sparse Core Ops, SparseCore 0:
  128.6 122.2 all-reduce.7
  290.7 119.7 all-reduce.9
  557.7 221.2 all-reduce.13
  783.2 237.2 all-reduce.11
where the time goes:
time: 1100 us; the launch traced here: 1090 us
  waiting for transfers between devices  586 us (53%)
  matrix products  205 us (19%)
  other arithmetic  164 us (15%)
  blocking collectives  80.9 us (7%)
  local copies, waits for them, and re-layouts  31.8 us (3%)
  between operations  24.1 us (2%)
    psum x1, waiting for transfers between devices, local(): lax.psum(jnp.dot(gated, down_low, preferred_element_type=jnp.float32), 'mp')  184 us
    psum x1, waiting for transfers between devices, local(): summed = lax.psum((grad_qkv, grad_outw, grad_up, grad_down), 'dp')  171 us
    psum x1, waiting for transfers between devices, local(): lax.psum(jnp.dot(mixed, out_low, preferred_element_type=jnp.float32), 'mp')  122 us
    psum x1, waiting for transfers between devices, local(): lax.psum(jnp.einsum('sf,df->sd', grad_upper, up_low, preferred_element_ty...  109 us
    psum x1, blocking collectives, local(): count, attn_total, mlp_total = lax.psum((count_here, attn_sq, mlp_sq), 'dp')  41.8 us
    psum x1, blocking collectives, local(): sq_total = lax.psum(raw_sq, ('dp', 'mp'))  39.1 us
    convert_element_type x4, other arithmetic, local(): grad_scores = (probs_full * (grad_probs - delta)).astype(jnp.bfloat16)  33.6 us
    dot_general x4, matrix products, local(): jnp.einsum('qhd,khd->hqk', grad_block, v_in, preferred_element_type=jnp.f...  32.5 us
  transfers between devices with their start and end apart: 4, of which 4 were waited for; matrix products, arithmetic and copies ran while one was open for 7% of the time, Pallas kernels for 0%

commit v1 on v0

--- a/solution.py
+++ b/solution.py
@@ -222,7 +222,7 @@
     raw_sq = (
         big_sq + jnp.where(first_dp, split_sq, 0.0) + jnp.where(first_dp & first_mp, whole_sq, 0.0)
     )
-    sq_total = lax.psum(raw_sq, ("dp", "mp"))
+    sq_total = lax.psum(lax.psum(raw_sq, "mp"), "dp")
     scale = seq_len * lax.axis_size("dp") / count
     grad_norm = scale * jnp.sqrt(sq_total)
     factor = jnp.minimum(1.0, CLIP_LIMIT / (grad_norm + 1e-06)) * scale

time: 1100 us -> 1100 us (level)
  blocking collectives: 80.9 us -> 68.6 us
  waiting for transfers between devices: 586 us -> 598 us
    psum x1, blocking collectives: 41.8 us -> 20 us  [local(): count, attn_total, mlp_total = lax.psum((count_here, attn_sq, mlp_sq), 'dp')]
    psum x1, waiting for transfers between devices: 171 us -> 184 us  [local(): summed = lax.psum((grad_qkv, grad_outw, grad_up, grad_down), 'dp')]
    psum x1 -> x2, blocking collectives: 39.1 us -> 48.6 us  [the longest x1 41.2 us: local(): lax.psum((vec_grad, head_grad, grad_bup), 'dp')]
  transfers between devices with their start and end apart: 4 -> 4, of which waited for: 4 -> 4; matrix products, arithmetic and copies ran while one was open for 7% -> 6% of each run, Pallas kernels for 0% -> 0%
where the time goes in v1:
time: 1100 us; the launch traced here: 1090 us
  waiting for transfers between devices  598 us (54%)
  matrix products  205 us (19%)
  other arithmetic  162 us (15%)
  blocking collectives  68.6 us (6%)
  local copies, waits for them, and re-layouts  34.7 us (3%)
  between operations  24.1 us (2%)
    psum x1, waiting for transfers between devices, local(): summed = lax.psum((grad_qkv, grad_outw, grad_up, grad_down), 'dp')  184 us
    psum x1, waiting for transfers between devices, local(): lax.psum(jnp.dot(gated, down_low, preferred_element_type=jnp.float32), 'mp')  184 us
    psum x1, waiting for transfers between devices, local(): lax.psum(jnp.dot(mixed, out_low, preferred_element_type=jnp.float32), 'mp')  122 us
    psum x1, waiting for transfers between devices, local(): lax.psum(jnp.einsum('sf,df->sd', grad_upper, up_low, preferred_element_ty...  109 us
    psum x1, blocking collectives, local(): lax.psum((vec_grad, head_grad, grad_bup), 'dp')  41.2 us
    convert_element_type x4, other arithmetic, local(): grad_scores = (probs_full * (grad_probs - delta)).astype(jnp.bfloat16)  33.6 us
    dot_general x4, matrix products, local(): jnp.einsum('qhd,khd->hqk', grad_block, v_in, preferred_element_type=jnp.f...  32.5 us
    reduce_sum x4, other arithmetic, local(): total = jnp.sum(expo, axis=-1, keepdims=True)  31.1 us
  transfers between devices with their start and end apart: 4, of which 4 were waited for; matrix products, arithmetic and copies ran while one was open for 6% of the time, Pallas kernels for 0%

profile of v1, /device:TPU:0, one launch (start us, length us, event | category | flops | bytes accessed | tf_op | source)
XLA Modules:
  0.0 1093.1 jit_solution(7242703862191913716)
XLA Ops:
  9.6 2.5 convert_reduce_fusion
  12.1 2.9 fusion.25
  15.8 2.3 fusion.148
  31.2 2.0 multiply_convert_fusion.6
  33.1 6.5 fusion.61
  39.7 6.6 select_reduce_fusion
  46.4 6.6 select_reduce_fusion.1
  53.0 7.8 fusion.3
  60.9 6.6 fusion.97
  67.5 7.8 fusion.2
  75.3 6.4 fusion.96
  81.7 6.7 select_reduce_fusion.2
  88.4 7.8 fusion.1
  96.2 6.6 fusion.95
  102.9 6.8 select_reduce_fusion.3
  109.6 7.8 fusion
  117.4 6.5 fusion.94
  124.9 3.6 fusion.126
  128.6 122.4 %all-reduce.9.cloned.1.call-done = f32[2048,768]{1,0:T(8,128)} async-done(((f32[2048,768]{1,0:T(8,128)}), f32[2048,768]{1,0:T(8,128)}) %all-reduce.9.cloned.1.call-update) | async-done | bytes 6291472 | tf_op jit(solution)/shard_map/psum | solution.py:116
  251.0 3.7 fusion.159
  258.5 17.7 %multiply_convert_fusion.4 = (bf16[2048,768]{1,0:T(8,128)(2,1)}, f32[2048,768]{1,0:T(8,128)}, f32[2048,768]{1,0:T(8,128)}) fusion(f32[768]{0:T(1024)S(1)} %copy-done.101, bf16[2048,768]{1,0:T(8,128)(2,1)S(1)} %add_convert_fusion.2, f32[768,768]{1,0:T(8,128)S(1)} %copy-done.81), kind=kOutput, calls=%fused_computation.76 | convolution fusion | flops 2520317952 | bytes 21236736 | tf_op jit(solution)/shard_map/dot_general | solution.py:122
  276.2 8.2 convert_reduce_fusion.3
  286.0 4.5 fusion.105
  293.8 8.1 fusion.101
  301.9 108.6 %all-reduce.11.cloned.1.call-done = f32[2048,768]{1,0:T(8,128)} async-done(((f32[2048,768]{1,0:T(8,128)}), f32[2048,768]{1,0:T(8,128)}) %all-reduce.11.cloned.1.call-update) | async-done | bytes 6291472 | tf_op jit(solution)/shard_map/psum | solution.py:142
  410.5 6.8 multiply_reduce_fusion.4
  417.3 6.5 convert_reduce_fusion.2
  426.7 6.8 multiply_reduce_fusion.3
  433.6 10.1 multiply_convert_fusion.3
  443.7 5.0 fusion.164
  448.7 3.3 fusion.121
  452.1 4.3 fusion.30
  456.4 9.1 multiply_reduce_fusion.2
  465.5 5.8 fusion.28
  471.3 7.4 multiply_reduce_fusion.1
  478.7 10.3 fusion.76
  489.0 9.2 multiply_reduce_fusion
  498.2 5.9 fusion.82
  504.1 9.5 multiply_convert_fusion
  513.7 5.7 fusion.167
  519.3 10.3 multiply_convert_fusion.2
  529.6 2.8 fusion.165
  532.4 4.0 convolution_add_fusion.2
  536.5 3.6 multiply_convert_fusion.1
  540.2 2.0 fusion.166
  545.1 2.6 multiply_reduce_fusion.9
  548.8 3.3 fusion.85
  553.0 4.5 convolution_bitcast_fusion
  557.9 7.1 fusion.168
  565.0 4.2 fusion.144
  572.1 3.6 fusion.87
  580.1 2.0 constant_dynamic-slice_fusion
  589.2 2.6 multiply_reduce_fusion.10
  592.5 2.1 convert_reduce_fusion.4
  595.3 183.7 %all-reduce.15.cloned.1.call-done = (f32[2048,768]{1,0:T(8,128)}, f32[2048,768]{1,0:T(8,128)}) async-done(((f32[2048,768]{1,0:T(8,128)}, f32[2048,768]{1,0:T(8,128)}), (f32[2048,768]{1,0:T(8,128)}, f32[2048,768]{1,0:T(8,128)})) %all-reduce.15.cloned.1.call-update) | async-done | bytes 12582928 | tf_op jit(solution)/shard_map/psum | solution.py:127
  779.0 13.3 %fusion.24 = (f32[768]{0:T(1024)S(1)}, f32[2048]{0:T(1024)S(1)}, f32[2048]{0:T(1024)S(1)}, f32[768]{0:T(1024)S(1)}, bf16[1,2048,768]{2,1,0:T(8,128)(2,1)}, /*index=5*/f32[]{:T(128)}, f32[768]{0:T(1024)S(1)}, f32[]{:T(128)}) fusion(f32[2048,768]{1,0:T(8,128)} %get-tuple-element.84, bf16[1,2048,768]{2,1,0:T(8,128)(2,1)S(1)} %copy-done.6, ...), kind=kLoop, calls=%fused_computation.53 | loop fusion | flops 39315200 | bytes 34662408 | tf_op jit(solution)/shard_map/reduce_sum | solution.py:193
  792.4 41.2 %all-reduce.1 = (f32[5,3,64]{2,1,0:T(4,128)S(1)}, f32[768]{0:T(1024)S(1)}, f32[6,768]{1,0:T(8,128)S(1)}) all-reduce(f32[5,3,64]{2,1,0:T(4,128)S(1)} %pad_maximum_fusion.3, f32[768]{0:T(1024)} %get-tuple-element.150, f32[6,768]{1,0:T(8,128)S(1)} %stack.49), channel_id=1, replica_groups=mesh['dp'=8,'mp'=4] {'dp'}, use_global_device_ids=true, to_apply=%region_45.46 | all-reduce | flops 6336 | bytes 50688 | tf_op jit(solution)/shard_map/psum | solution.py:200
  837.4 183.7 %all-reduce.13.cloned.1.call-done = (f32[3,768,192]{1,2,0:T(8,128)}, f32[192,768]{1,0:T(8,128)}, f32[768,768]{1,0:T(8,128)}, f32[768,768]{0,1:T(8,128)}) async-done(((f32[3,768,192]{1,2,0:T(8,128)}, f32[192,768]{1,0:T(8,128)}, f32[768,768]{1,0:T(8,128)}, f32[768,768]{0,1:T(8,128)}), (f32[3,768,192]{1,2,0:T(8,128)}, f32[192,768]{1,0:T(8,128)}, f32[768,768]{1,0:T(8,128)}, ...) | async-done | bytes 7077904 | tf_op jit(solution)/shard_map/psum | solution.py:204
  1030.5 7.4 psum.124
  1037.9 20.0 %all-reduce = (f32[]{:T(128)}, f32[]{:T(128)}, f32[1]{0:T(128)}, f32[1]{0:T(128)}) all-reduce(f32[]{:T(128)} %convert_reduce_fusion.5, f32[]{:T(128)} %psum.124, f32[1]{0:T(128)} %bitcast.52, f32[1]{0:T(128)} %bitcast.51), channel_id=1, replica_groups=mesh['dp'=8,'mp'=4] {'dp'}, use_global_device_ids=true, to_apply=%region_33.34 | all-reduce | flops 4 | bytes 32 | tf_op jit(solution)/shard_map/psum | solution.py:133
  1059.9 2.5 multiply_subtract_fusion.2
  1067.9 2.3 multiply_subtract_fusion.1
  1072.3 7.0 fusion.71
  1081.3 2.0 multiply_subtract_fusion
  (351 shorter events, 68.7 us)
Async XLA Ops:
  7.2 8.6 copy-start.5
  7.2 7.8 copy-start.66
  7.2 243.7 %all-reduce.9.cloned.1.call-start = ((), (), s32[]{:S(2)}) async-start(), calls=%async_computation | async-start | bytes 12582912 | tf_op jit(solution)/shard_map/psum | solution.py:116
  9.5 21.7 %copy-start.68 = (f32[3,64]{1,0:T(4,128)}, f32[3,64]{1,0:T(4,128)S(1)}, u32[]{:S(2)}) copy-start(f32[3,64]{1,0:T(4,128)S(1)} %get-tuple-element.123) | copy-start | bytes 2308
  15.7 235.3 %copy-start.82 = (f32[768]{0:T(1024)}, f32[768]{0:T(1024)S(1)}, u32[]{:S(2)}) copy-start(f32[768]{0:T(1024)S(1)} %get-tuple-element.66) | copy-start | bytes 9220
  24.5 15.2 %copy-start.56 = (f32[2048,3]{0,1:T(4,128)}, f32[2048,3]{0,1:T(4,128)S(1)}, u32[]{:S(2)}) copy-start(f32[2048,3]{0,1:T(4,128)S(1)} %broadcast_multiply_fusion.5) | copy-start | bytes 73732
  26.2 20.2 %copy-start.58 = (f32[2048,3]{0,1:T(4,128)}, f32[2048,3]{0,1:T(4,128)S(1)}, u32[]{:S(2)}) copy-start(f32[2048,3]{0,1:T(4,128)S(1)} %add_rsqrt_fusion.1) | copy-start | bytes 73732
  27.8 18.6 %copy-start.48 = (f32[2048,3]{0,1:T(4,128)}, f32[2048,3]{0,1:T(4,128)S(1)}, u32[]{:S(2)}) copy-start(f32[2048,3]{0,1:T(4,128)S(1)} %broadcast_multiply_fusion.4) | copy-start | bytes 73732
  29.4 16.9 %copy-start.50 = (f32[2048,3]{0,1:T(4,128)}, f32[2048,3]{0,1:T(4,128)S(1)}, u32[]{:S(2)}) copy-start(f32[2048,3]{0,1:T(4,128)S(1)} %add_rsqrt_fusion) | copy-start | bytes 73732
  31.2 71.7 %copy-start.29 = (bf16[2048,3,64]{0,2,1:T(8,128)(2,1)}, bf16[2048,3,64]{0,2,1:T(8,128)(2,1)S(1)}, u32[]{:S(2)}) copy-start(bf16[2048,3,64]{0,2,1:T(8,128)(2,1)S(1)} %multiply_convert_fusion.7) | copy-start | bytes 2359300
  33.1 69.7 %copy-start.2 = (bf16[2048,3,64]{0,2,1:T(8,128)(2,1)}, bf16[2048,3,64]{0,2,1:T(8,128)(2,1)S(1)}, u32[]{:S(2)}) copy-start(bf16[2048,3,64]{0,2,1:T(8,128)(2,1)S(1)} %multiply_convert_fusion.6) | copy-start | bytes 2359300
  39.7 21.2 %copy-start.13 = (pred[512,2048]{1,0:T(8,128)(4,1)}, pred[512,2048]{1,0:T(8,128)(4,1)S(1)}, u32[]{:S(2)}) copy-start(pred[512,2048]{1,0:T(8,128)(4,1)S(1)} %get-tuple-element.127) | copy-start | bytes 3145732
  39.7 35.6 %copy-start.7 = (pred[512,2048]{1,0:T(8,128)(4,1)}, pred[512,2048]{1,0:T(8,128)(4,1)S(1)}, u32[]{:S(2)}) copy-start(pred[512,2048]{1,0:T(8,128)(4,1)S(1)} %get-tuple-element.126) | copy-start | bytes 3145732
  39.7 56.5 %copy-start.10 = (pred[512,2048]{1,0:T(8,128)(4,1)}, pred[512,2048]{1,0:T(8,128)(4,1)S(1)}, u32[]{:S(2)}) copy-start(pred[512,2048]{1,0:T(8,128)(4,1)S(1)} %get-tuple-element.125) | copy-start | bytes 3145732
  39.7 77.7 %copy-start.15 = (pred[512,2048]{1,0:T(8,128)(4,1)}, pred[512,2048]{1,0:T(8,128)(4,1)S(1)}, u32[]{:S(2)}) copy-start(pred[512,2048]{1,0:T(8,128)(4,1)S(1)} %get-tuple-element.124) | copy-start | bytes 3145732
  46.4 14.5 %copy-start.75 = (f32[3,512]{1,0:T(4,128)}, f32[3,512]{1,0:T(4,128)S(1)}, u32[]{:S(2)}) copy-start(f32[3,512]{1,0:T(4,128)S(1)} %get-tuple-element.132) | copy-start | bytes 18436
  53.0 7.9 copy-start.20
  117.4 7.5 copy-start.42
  128.5 282.0 %all-reduce.11.cloned.1.call-start = ((), (), s32[]{:S(2)}) async-start(), calls=%async_computation.1 | async-start | bytes 12582912 | tf_op jit(solution)/shard_map/psum | solution.py:142
  128.6 288.7 %copy-start.72 = (f32[1,2048]{1,0:T(1,128)}, f32[1,2048]{1,0:T(1,128)S(1)}, u32[]{:S(2)}) copy-start(f32[1,2048]{1,0:T(1,128)S(1)} %convert_element_type.148) | copy-start | bytes 24580
  258.5 17.7 %copy-start.41 = (bf16[2048,768]{1,0:T(8,128)(2,1)}, bf16[2048,768]{1,0:T(8,128)(2,1)S(1)}, u32[]{:S(2)}) copy-start(bf16[2048,768]{1,0:T(8,128)(2,1)S(1)} %add_convert_fusion.2) | copy-start | bytes 9437188
  258.5 17.7 %copy-start.25 = (bf16[1,2048,768]{2,1,0:T(8,128)(2,1)S(1)}, bf16[1,2048,768]{2,1,0:T(8,128)(2,1)}, u32[]{:S(2)}) copy-start(bf16[1,2048,768]{2,1,0:T(8,128)(2,1)} %param.27) | copy-start | bytes 9437188
  258.5 17.7 %copy-start.77 = (f32[768,768]{1,0:T(8,128)S(1)}, f32[768,768]{1,0:T(8,128)}, u32[]{:S(2)}) copy-start(f32[768,768]{1,0:T(8,128)} %param.40) | copy-start | bytes 7077892
  290.6 488.4 %all-reduce.15.cloned.1.call-start = ((), (), s32[]{:S(2)}) async-start(), calls=%async_computation.3 | async-start | bytes 25165824 | tf_op jit(solution)/shard_map/psum | solution.py:127
  293.8 139.8 %copy-start.61 = (f32[3,512]{1,0:T(4,128)}, f32[3,512]{1,0:T(4,128)S(1)}, u32[]{:S(2)}) copy-start(f32[3,512]{1,0:T(4,128)S(1)} %log_add_fusion.3) | copy-start | bytes 18436
  417.3 9.4 slice-start.9
  417.3 9.4 slice-start.10
  417.3 9.4 slice-start.11
  425.8 7.8 copy-start.45
  426.7 25.3 %slice-start.6 = ((s8[12582912]{0:T(1024)(128)(4,1)}), s8[4194304]{0:T(1024)(128)(4,1)S(1)}, s32[]{:S(2)}) async-start(s8[12582912]{0:T(1024)(128)(4,1)} %bitcast.194), calls=%async_computation.10 | async-start | bytes 8388608
  426.7 25.3 %slice-start.7 = ((s8[12582912]{0:T(1024)(128)(4,1)}), s8[4194304]{0:T(1024)(128)(4,1)S(1)}, s32[]{:S(2)}) async-start(s8[12582912]{0:T(1024)(128)(4,1)} %bitcast.194), calls=%async_computation.11 | async-start | bytes 8388608
  433.6 10.1 copy-start.3
  433.6 18.5 %slice-start.8 = ((s8[12582912]{0:T(1024)(128)(4,1)}), s8[4194304]{0:T(1024)(128)(4,1)S(1)}, s32[]{:S(2)}) async-start(s8[12582912]{0:T(1024)(128)(4,1)} %bitcast.194), calls=%async_computation.12 | async-start | bytes 8388608
  443.7 8.3 copy-start.11
  443.7 8.3 copy-start.47
  452.1 13.4 %slice-start = ((s8[12582912]{0:T(1024)(128)(4,1)}), s8[4194304]{0:T(1024)(128)(4,1)S(1)}, s32[]{:S(2)}) async-start(s8[12582912]{0:T(1024)(128)(4,1)} %bitcast.190), calls=%async_computation.4 | async-start | bytes 8388608
  456.4 9.1 slice-start.1
  456.4 9.1 slice-start.2
  471.3 17.7 %slice-start.3 = ((s8[12582912]{0:T(1024)(128)(4,1)}), s8[4194304]{0:T(1024)(128)(4,1)S(1)}, s32[]{:S(2)}) async-start(s8[12582912]{0:T(1024)(128)(4,1)} %bitcast.192), calls=%async_computation.7 | async-start | bytes 8388608
  471.3 17.7 %slice-start.4 = ((s8[12582912]{0:T(1024)(128)(4,1)}), s8[4194304]{0:T(1024)(128)(4,1)S(1)}, s32[]{:S(2)}) async-start(s8[12582912]{0:T(1024)(128)(4,1)} %bitcast.192), calls=%async_computation.8 | async-start | bytes 8388608
  478.7 10.3 slice-start.5
  504.1 9.6 copy-start.4
  519.3 17.2 %slice-start.14 = ((s8[12582912]{0:T(1024)(128)(4,1)}), s8[4194304]{0:T(1024)(128)(4,1)S(1)}, s32[]{:S(2)}) async-start(s8[12582912]{0:T(1024)(128)(4,1)} %bitcast.200), calls=%async_computation.18 | async-start | bytes 8388608
  519.3 17.2 %slice-start.15 = ((s8[12582912]{0:T(1024)(128)(4,1)}), s8[4194304]{0:T(1024)(128)(4,1)S(1)}, s32[]{:S(2)}) async-start(s8[12582912]{0:T(1024)(128)(4,1)} %bitcast.200), calls=%async_computation.19 | async-start | bytes 8388608
  557.6 7.4 copy-start.26
  557.6 7.4 copy-start.73
  557.6 463.5 %all-reduce.13.cloned.1.call-start = ((), (), s32[]{:S(2)}) async-start(), calls=%async_computation.2 | async-start | bytes 14155776 | tf_op jit(solution)/shard_map/psum | solution.py:204
  557.9 11.3 %slice-start.12 = ((s8[6291456]{0:T(1024)(128)(4,1)}), s8[4194304]{0:T(1024)(128)(4,1)S(1)}, s32[]{:S(2)}) async-start(s8[6291456]{0:T(1024)(128)(4,1)} %bitcast.198), calls=%async_computation.16 | async-start | bytes 8388608
  779.0 13.3 %copy-start.93 = (f32[1,768]{1,0:T(1,128)S(1)}, f32[1,768]{1,0:T(1,128)}, u32[]{:S(2)}) copy-start(f32[1,768]{1,0:T(1,128)} %stack.45) | copy-start | bytes 9220
  779.0 13.4 %copy-start.94 = (f32[1,768]{1,0:T(1,128)S(1)}, f32[1,768]{1,0:T(1,128)}, u32[]{:S(2)}) copy-start(f32[1,768]{1,0:T(1,128)} %stack.46) | copy-start | bytes 9220
  779.0 13.4 %copy-start.95 = (f32[1,768]{1,0:T(1,128)S(1)}, f32[1,768]{1,0:T(1,128)}, u32[]{:S(2)}) copy-start(f32[1,768]{1,0:T(1,128)} %stack.47) | copy-start | bytes 9220
  779.0 280.9 %copy-start.52 = (f32[3,96,192]{1,2,0:T(8,128)S(1)}, f32[3,96,192]{1,2,0:T(8,128)}, u32[]{:S(2)}) copy-start(f32[3,96,192]{1,2,0:T(8,128)} %copy.51) | copy-start | bytes 663556
  833.6 236.5 %copy-start.91 = (f32[768]{0:T(1024)}, f32[768]{0:T(1024)S(1)}, u32[]{:S(2)}) copy-start(f32[768]{0:T(1024)S(1)} %get-tuple-element.77) | copy-start | bytes 9220
  1072.1 7.2 copy-start.103
  1072.2 7.2 copy-start.104
  1072.2 7.8 copy-start.78
  1072.2 7.8 copy-start.96
  1072.2 7.8 copy-start.97
  1072.2 8.4 copy-start.67
  1072.2 8.4 copy-start.89
  1072.2 8.4 copy-start.90
  1072.2 9.0 copy-start.53
  1072.2 9.0 copy-start.62
  1072.3 9.0 copy-start.63
  (68 other events, 255.9 us)
Sparse Core Ops, SparseCore 0:
  128.7 122.2 all-reduce.8
  290.7 119.7 all-reduce.10
  557.7 221.2 all-reduce.14
  783.8 237.2 all-reduce.12
